TPU v7x, 256 devices: a whole 4x4x8 slice. The times are simulated.
256 devices in a mesh: gx: 32 (over y_lo, z, core), gy: 8 (over x, y_hi).
Axes of the slice: x: 4, y: 4 (y_hi: 2, y_lo: 2; y = y_hi * 2 + y_lo), z: 8, core: 2. Of those that a mesh axis runs over, the one named last changes fastest.
Arguments:
- features: bfloat16 [8192, 32, 8, 256], P('gx', 'gy'), may hold values from -6 to 6
- spectral_weight: bfloat16 [16, 2, 256, 256], replicated, may hold values from -6 to 6
- conv_taps: float32 [3, 256], replicated, may hold values from -3 to 3
- w_in: bfloat16 [256, 1024], replicated, may hold values from -0.375 to 0.375
- bias_in: float32 [1024], replicated, may hold values from -3 to 3
- w_out: bfloat16 [1024, 256], replicated, may hold values from -0.1875 to 0.1875
- bias_out: float32 [256], replicated, may hold values from -3 to 3
Outputs:
- layer_out: bfloat16 [8192, 32, 8, 256], P('gx', 'gy')
All inputs are finite; a program needn't handle non-finite values.
Results may differ from a plain program's by a relative error of at most 0.0065.
Values may be sent and summed in bfloat16 or wider, within the bound.
A program may use at most 128 MiB of HBM per device.

v0:
```python
import math

import jax
import jax.numpy as jnp
from jax import lax
from jax.sharding import PartitionSpec as P


def with_halo(cells, sides, width):
    for axis, dim in sides:
        count = lax.axis_size(axis)
        ends = count - 1
        head = lax.slice_in_dim(cells, 0, width, axis=dim)
        tail = lax.slice_in_dim(cells, cells.shape[dim] - width, cells.shape[dim], axis=dim)
        cells = jnp.concatenate(
            [
                lax.ppermute(tail, axis, [(i, (i + 1) % count) for i in range(ends)]),
                cells,
                lax.ppermute(head, axis, [((i + 1) % count, i) for i in range(ends)]),
            ],
            axis=dim,
        )
    return cells


def cut_along(value, dim, peers):
    shape = value.shape
    parts = value.reshape(*shape[:dim], peers, shape[dim] // peers, *shape[dim + 1 :])
    return jnp.moveaxis(parts, dim, 0)


def sum_at_owner(value, axis, dim):
    peers = lax.axis_size(axis)
    parts = lax.all_to_all(cut_along(value, dim, peers), axis, 0, 0, tiled=True)
    return jnp.sum(parts, axis=0)


def copy_for_each(value, axis):
    copies = jnp.broadcast_to(value, (lax.axis_size(axis), *value.shape))
    return lax.all_to_all(copies, axis, split_axis=0, concat_axis=0, tiled=True)


def joined_along(parts, dim):
    parts = jnp.moveaxis(parts, 0, dim)
    shape = parts.shape
    return parts.reshape(*shape[:dim], shape[dim] * shape[dim + 1], *shape[dim + 2 :])


def collect(value, axis, dim):
    parts = copy_for_each(value, axis)
    return joined_along(parts, dim)


def make_tables(positions, total, mode_count):
    waves = jnp.arange(mode_count, dtype=jnp.int32)
    product = waves[:, None] * positions[None, :] % total
    angles = 2.0 * math.pi / total * product.astype(jnp.float32)
    scale = 1.0 / math.sqrt(total)
    cosines = jnp.cos(angles)
    sines = jnp.sin(angles)
    forward = (jnp.concatenate([cosines, -sines], 0) * scale).astype(jnp.bfloat16)
    amplitude = jnp.where(waves == 0, 1.0, 2.0).astype(jnp.float32)[:, None]
    inverse = (jnp.concatenate([amplitude * cosines, -amplitude * sines], 0) * scale).T.astype(
        jnp.bfloat16
    )
    return (forward, inverse)


def local(features, spectral_weight, conv_taps, w_in, bias_in, w_out, bias_out):
    x_rows, y_rows, z_cols, channels = features.shape
    gx_size = lax.axis_size("gx")
    mode_count = spectral_weight.shape[0]
    positions = lax.axis_index("gx") * x_rows + jnp.arange(x_rows, dtype=jnp.int32)
    forward, inverse = make_tables(positions, x_rows * gx_size, mode_count)
    col_count = features.shape[2]
    row_count = y_rows * col_count
    padded = with_halo(features, (("gy", 1),), 1)
    flattened = features.reshape(x_rows, row_count * channels)
    spectrum = jnp.dot(forward, flattened, preferred_element_type=jnp.float32)
    spectrum = spectrum.reshape(2, mode_count * row_count, channels)
    owned = sum_at_owner(spectrum, "gx", 1).astype(jnp.bfloat16)
    per_mode = gx_size // mode_count
    owner_mode = lax.axis_index("gx") // per_mode
    chosen = lax.dynamic_index_in_dim(spectral_weight, owner_mode, 0, keepdims=False)
    mixed_real = jnp.dot(owned[0], chosen[0], preferred_element_type=jnp.float32) - jnp.dot(
        owned[1], chosen[1], preferred_element_type=jnp.float32
    )
    mixed_imag = jnp.dot(owned[0], chosen[1], preferred_element_type=jnp.float32) + jnp.dot(
        owned[1], chosen[0], preferred_element_type=jnp.float32
    )
    mixed_own = jnp.stack([mixed_real, mixed_imag]).astype(jnp.bfloat16)
    mixed = collect(mixed_own, "gx", 1)
    mixed = mixed.reshape(2 * mode_count, row_count * channels)
    spectral = jnp.dot(inverse, mixed, preferred_element_type=jnp.float32)
    spectral = spectral.reshape(x_rows, y_rows, col_count, channels)
    conv = (
        conv_taps[0] * padded[:, :-2].astype(jnp.float32)
        + conv_taps[1] * padded[:, 1:-1].astype(jnp.float32)
        + conv_taps[2] * padded[:, 2:].astype(jnp.float32)
    )
    joined = (spectral + conv).astype(jnp.bfloat16).reshape(x_rows * row_count, channels)
    hidden = jax.nn.gelu(
        jnp.dot(joined, w_in, preferred_element_type=jnp.float32) + bias_in, approximate=True
    ).astype(jnp.bfloat16)
    result = (
        features.reshape(x_rows * row_count, channels).astype(jnp.float32)
        + jnp.dot(hidden, w_out, preferred_element_type=jnp.float32)
        + bias_out
    )
    return result.astype(jnp.bfloat16).reshape(x_rows, y_rows, col_count, channels)


def solution(mesh):
    return jax.shard_map(
        local,
        mesh=mesh,
        in_specs=(P("gx", "gy", None, None), P(), P(), P(), P(), P(), P()),
        out_specs=P("gx", "gy", None, None),
        check_vma=False,
    )
```

profile of v0, /device:TPU:6, one launch (start us, length us, event | category | flops | bytes accessed | tf_op | source)
XLA Modules:
  0.0 120.0 jit_solution(2121349210019286884)
XLA Ops:
  0.0 6.5 %copy.32 = bf16[32,8,32,256]{3,1,2,0:T(8,128)(2,1)S(1)} copy(bf16[32,8,32,256]{3,2,1,0:T(8,128)(2,1)} %bitcast.51) | data formatting | bytes 8388608
  6.7 0.8 fusion.36
  7.5 0.2 reshape_reshape.6
  7.6 1.2 copy.41
  8.8 9.9 %all-to-all-start = ((f32[32,2,16,256]{3,2,1,0:T(8,128)}), f32[32,2,16,256]{3,2,1,0:T(8,128)S(1)}, u32[]{:S(2)}, u32[]{:S(2)}) async-start(f32[32,2,16,256]{3,2,1,0:T(8,128)} %bitcast.49), calls=%async_computation | async-start | bytes 2097152 | tf_op jit(solution)/shard_map/all_to_all | solution.py:34
  18.7 8.0 %fusion.62 = (bf16[256,4,8,256]{3,0,2,1:T(8,128)(2,1)S(1)}, f32[256,4,8,256]{3,0,2,1:T(8,128)}) fusion(bf16[256,4,8,256]{3,2,1,0:T(8,128)(2,1)} %param.7), kind=kLoop, calls=%fused_computation.72 | loop fusion | flops 2097152 | bytes 16777216 | tf_op args[0]
  26.7 2.0 %copy-done.1 = bf16[256,4,8,256]{3,0,2,1:T(8,128)(2,1)} copy-done((bf16[256,4,8,256]{3,0,2,1:T(8,128)(2,1)}, bf16[256,4,8,256]{3,0,2,1:T(8,128)(2,1)S(1)}, u32[]{:S(2)}) %copy-start.1) | copy-done | bytes 4194328
  28.7 1.2 fusion.61
  29.9 4.8 %collective-permute-start = (bf16[256,1,8,256]{3,0,2,1:T(8,128)(2,1)}, bf16[256,1,8,256]{3,0,2,1:T(8,128)(2,1)}, u32[]{:S(2)}, u32[]{:S(2)}) collective-permute-start(bf16[256,1,8,256]{3,0,2,1:T(8,128)(2,1)} %get-tuple-element.5), channel_id=1, source_target_pairs={{0,1},{1,2},{2,3},{3,4},{4,5},{5,6},{6,7},{8,9},{9,10},{10,11},{11... | collective-permute-start | bytes 3145736 | tf_op jit(solution)/shard_map/ppermute | solution.py:17
  34.7 3.4 %collective-permute-start.1 = (bf16[256,1,8,256]{3,0,2,1:T(8,128)(2,1)S(1)}, bf16[256,1,8,256]{3,0,2,1:T(8,128)(2,1)}, u32[]{:S(2)}, u32[]{:S(2)}) collective-permute-start(bf16[256,1,8,256]{3,0,2,1:T(8,128)(2,1)S(1)} %get-tuple-element.6), channel_id=1, source_target_pairs={{1,0},{2,1},{3,2},{4,3},{5,4},{6,5},{7,6},{9,8},{10,9},{11,10},{12... | collective-permute-start | bytes 3145736 | tf_op jit(solution)/shard_map/ppermute | solution.py:19
  38.2 9.0 %all-to-all-done = f32[32,2,16,256]{3,2,1,0:T(8,128)S(1)} async-done(((f32[32,2,16,256]{3,2,1,0:T(8,128)}), f32[32,2,16,256]{3,2,1,0:T(8,128)S(1)}, u32[]{:S(2)}, u32[]{:S(2)}) %all-to-all-start) | async-done | bytes 1048608 | tf_op jit(solution)/shard_map/all_to_all | solution.py:34
  47.2 1.0 fusion.29
  48.3 1.1 fusion.30
  49.3 1.1 fusion.23
  50.4 1.1 fusion.24
  51.5 0.9 broadcast_in_dim.18
  52.3 4.2 %all-to-all-start.1 = ((bf16[32,2,16,256]{3,2,1,0:T(8,128)(2,1)}), bf16[32,2,16,256]{3,2,1,0:T(8,128)(2,1)S(1)}, u32[]{:S(2)}, u32[]{:S(2)}) async-start(bf16[32,2,16,256]{3,2,1,0:T(8,128)(2,1)} %broadcast_in_dim.18), calls=%async_computation.1 | async-start | bytes 1048576 | tf_op jit(solution)/shard_map/all_to_all | solution.py:40
  56.6 11.5 %copy.22 = f32[256,4,8,256]{3,2,1,0:T(8,128)} copy(f32[256,4,8,256]{3,0,2,1:T(8,128)} %get-tuple-element.8) | data formatting | bytes 16777216 | tf_op jit(solution)/shard_map/convert_element_type | solution.py:106
  68.1 6.7 %all-to-all-done.1 = bf16[32,2,16,256]{3,2,1,0:T(8,128)(2,1)S(1)} async-done(((bf16[32,2,16,256]{3,2,1,0:T(8,128)(2,1)}), bf16[32,2,16,256]{3,2,1,0:T(8,128)(2,1)S(1)}, u32[]{:S(2)}, u32[]{:S(2)}) %all-to-all-start.1) | async-done | bytes 524320 | tf_op jit(solution)/shard_map/all_to_all | solution.py:40
  74.8 0.2 reshape_reshape.7
  75.2 16.6 %collective-permute-done.1 = bf16[256,1,8,256]{3,0,2,1:T(8,128)(2,1)} collective-permute-done((bf16[256,1,8,256]{3,0,2,1:T(8,128)(2,1)S(1)}, bf16[256,1,8,256]{3,0,2,1:T(8,128)(2,1)}, u32[]{:S(2)}, u32[]{:S(2)}) %collective-permute-start.1) | collective-permute-done | bytes 1048608 | tf_op jit(solution)/shard_map/ppermute | solution.py:19
  91.8 6.9 %add_convert_fusion = bf16[256,4,8,256]{3,0,2,1:T(8,128)(2,1)S(1)} fusion(bf16[256,1,8,256]{3,0,2,1:T(8,128)(2,1)} %collective-permute-done.1, bf16[256,4,8,256]{3,0,2,1:T(8,128)(2,1)} %copy-done.1, bf16[256,1,8,256]{3,0,2,1:T(8,128)(2,1)} %collective-permute-done, f32[256]{0:T(256)S(1)} %bitcast.58, f32[256]{0:T(256)S(1)} %bitcast.59, ...), kind=kOutput, calls=%fused_computation.14 | convolution fusion | flops 159408128 | bytes 11045888 | tf_op jit(solution)/shard_map/dot_general | solution.py:94
  98.7 4.4 %copy.30 = bf16[256,4,8,256]{3,2,1,0:T(8,128)(2,1)} copy(bf16[256,4,8,256]{3,0,2,1:T(8,128)(2,1)S(1)} %add_convert_fusion) | data formatting | bytes 8388608 | tf_op jit(solution)/shard_map/convert_element_type | solution.py:101
  103.1 16.9 %fusion.16 = bf16[8192,256]{1,0:T(8,128)(2,1)} fusion(f32[8192,256]{1,0:T(8,128)} %bitcast.52, bf16[1024,256]{1,0:T(8,128)(2,1)S(1)} %copy-done, f32[1024]{0:T(1024)S(1)} %copy-done.4, bf16[8192,256]{1,0:T(8,128)(2,1)} %bitcast.53, bf16[256,1024]{1,0:T(8,128)(2,1)S(1)} %copy-done.3, f32[256]{0:T(256)S(1)} %copy-done.5), kind=kOutput, calls=%fused_computation.12 | convolution fusion | flops 8680112128 | bytes 17830912 | tf_op jit(solution)/shard_map/dot_general | solution.py:107
  (20 shorter events, 0.4 us)
Async XLA Ops:
  0.0 103.1 %copy-start = (bf16[1024,256]{1,0:T(8,128)(2,1)S(1)}, bf16[1024,256]{1,0:T(8,128)(2,1)}, u32[]{:S(2)}) copy-start(bf16[1024,256]{1,0:T(8,128)(2,1)} %param.12) | copy-start | bytes 1572868
  8.8 38.4 %all-to-all-start = ((f32[32,2,16,256]{3,2,1,0:T(8,128)}), f32[32,2,16,256]{3,2,1,0:T(8,128)S(1)}, u32[]{:S(2)}, u32[]{:S(2)}) async-start(f32[32,2,16,256]{3,2,1,0:T(8,128)} %bitcast.49), calls=%async_computation | async-start | bytes 2097152 | tf_op jit(solution)/shard_map/all_to_all | solution.py:34
  26.7 2.0 %copy-start.1 = (bf16[256,4,8,256]{3,0,2,1:T(8,128)(2,1)}, bf16[256,4,8,256]{3,0,2,1:T(8,128)(2,1)S(1)}, u32[]{:S(2)}) copy-start(bf16[256,4,8,256]{3,0,2,1:T(8,128)(2,1)S(1)} %get-tuple-element.7) | copy-start | bytes 12582916
  29.9 45.3 %collective-permute-start = (bf16[256,1,8,256]{3,0,2,1:T(8,128)(2,1)}, bf16[256,1,8,256]{3,0,2,1:T(8,128)(2,1)}, u32[]{:S(2)}, u32[]{:S(2)}) collective-permute-start(bf16[256,1,8,256]{3,0,2,1:T(8,128)(2,1)} %get-tuple-element.5), channel_id=1, source_target_pairs={{0,1},{1,2},{2,3},{3,4},{4,5},{5,6},{6,7},{8,9},{9,10},{10,11},{11... | collective-permute-start | bytes 3145736 | tf_op jit(solution)/shard_map/ppermute | solution.py:17
  34.7 57.1 %collective-permute-start.1 = (bf16[256,1,8,256]{3,0,2,1:T(8,128)(2,1)S(1)}, bf16[256,1,8,256]{3,0,2,1:T(8,128)(2,1)}, u32[]{:S(2)}, u32[]{:S(2)}) collective-permute-start(bf16[256,1,8,256]{3,0,2,1:T(8,128)(2,1)S(1)} %get-tuple-element.6), channel_id=1, source_target_pairs={{1,0},{2,1},{3,2},{4,3},{5,4},{6,5},{7,6},{9,8},{10,9},{11,10},{12... | collective-permute-start | bytes 3145736 | tf_op jit(solution)/shard_map/ppermute | solution.py:19
  52.3 22.5 %all-to-all-start.1 = ((bf16[32,2,16,256]{3,2,1,0:T(8,128)(2,1)}), bf16[32,2,16,256]{3,2,1,0:T(8,128)(2,1)S(1)}, u32[]{:S(2)}, u32[]{:S(2)}) async-start(bf16[32,2,16,256]{3,2,1,0:T(8,128)(2,1)} %broadcast_in_dim.18), calls=%async_computation.1 | async-start | bytes 1048576 | tf_op jit(solution)/shard_map/all_to_all | solution.py:40
  56.6 11.5 %copy-start.2 = (f32[3,256]{1,0:T(4,128)S(1)}, f32[3,256]{1,0:T(4,128)}, u32[]{:S(2)}) copy-start(f32[3,256]{1,0:T(4,128)} %param.9) | copy-start | bytes 9220
  98.7 4.4 %copy-start.3 = (bf16[256,1024]{1,0:T(8,128)(2,1)S(1)}, bf16[256,1024]{1,0:T(8,128)(2,1)}, u32[]{:S(2)}) copy-start(bf16[256,1024]{1,0:T(8,128)(2,1)} %param.10) | copy-start | bytes 1572868
  98.7 4.4 %copy-start.4 = (f32[1024]{0:T(1024)S(1)}, f32[1024]{0:T(1024)}, u32[]{:S(2)}) copy-start(f32[1024]{0:T(1024)} %param.11) | copy-start | bytes 12292
  98.7 4.4 %copy-start.5 = (f32[256]{0:T(256)S(1)}, f32[256]{0:T(256)}, u32[]{:S(2)}) copy-start(f32[256]{0:T(256)} %param.13) | copy-start | bytes 3076
where the time goes:
time: 121 us; the launch traced here: 120 us
  waiting for transfers between devices  32.3 us (27%)
  matrix products  28.8 us (24%)
  local copies, waits for them, and re-layouts  28.2 us (23%)
  starting transfers between devices  22.3 us (18%)
  other arithmetic  8.22 us (7%)
    dot_general x1, matrix products, local(): jnp.dot(hidden, w_out, preferred_element_type=jnp.float32)  16.9 us
    ppermute x1, waiting for transfers between devices, with_halo(): lax.ppermute(head, axis, [((i + 1) % count, i) for i in range(ends)])  16.6 us
    convert_element_type x1, local copies, waits for them, and re-layouts, local(): features.reshape(x_rows * row_count, channels).astype(jnp.float32)  11.5 us
    all_to_all x1, starting transfers between devices, sum_at_owner(): parts = lax.all_to_all(cut_along(value, dim, peers), axis, 0, 0, tiled=True)  9.86 us
    all_to_all x1, waiting for transfers between devices, sum_at_owner(): parts = lax.all_to_all(cut_along(value, dim, peers), axis, 0, 0, tiled=True)  9 us
    unnamed x14, local copies, waits for them, and re-layouts  8.68 us
    unnamed x1, other arithmetic  8.04 us
    dot_general x1, matrix products, local(): spectral = jnp.dot(inverse, mixed, preferred_element_type=jnp.float32)  6.89 us
  transfers between devices with their start and end apart: 4, of which 3 were waited for; matrix products, arithmetic and copies ran while one was open for 22% of the time, Pallas kernels for 0%

commit v1 on v0

v1 whole, which is shorter than its diff:
```python
import functools
import math

import jax
import jax.numpy as jnp
from jax import lax
from jax.experimental import pallas as pl
from jax.experimental.pallas import tpu as pltpu
from jax.sharding import PartitionSpec as P

MESH = pl.DeviceIdType.MESH
BF = jnp.bfloat16
F32 = jnp.float32
X = 8192
MODES = 16
XL = 256
YL = 4
Z = 8
C = 256
HID = 1024
NCH = 16
EARLY = 4
CROWS = XL // NCH
XB = 128
HB = 64
HC = 256


def table(shape, lane_is_mode):
    rows = lax.broadcasted_iota(jnp.int32, shape, 0)
    cols = lax.broadcasted_iota(jnp.int32, shape, 1)
    first = lax.axis_index("gx") * XL
    if lane_is_mode:
        mode, part, x = cols // 16, (cols // 8) % 2, first + rows
    else:
        mode, part, x = rows // 2, rows % 2, first + cols // 8
    turn = (mode * x + part * (X // 4)) % X
    value = jnp.cos((2.0 * math.pi / X) * turn.astype(F32)) * (1.0 / math.sqrt(X))
    if lane_is_mode:
        value = value * jnp.where(mode == 0, 1.0, 2.0)
    return value


def gelu_doubled(x):
    c = math.sqrt(2.0 / math.pi)
    t = jnp.tanh(x * (c + (c * 0.044715) * (x * x)))
    return x + x * t


def kernel(
    f_hbm, sw_hbm, taps_hbm, w1_hbm, b1_hbm, w2_hbm, b2_hbm,
    out,
    fv, fwd, inv, tab, tabt, s32, csend, crecv, zsend, zrecv, ysend, yrecv, wmix, mixed, mg, taps, w1, b1, w2, b2,
    fsem, wsem, hs, hr, cs, cr, zs, zr, ys, yr, gs, gr, ks, kr,
):
    gx, gy = lax.axis_index("gx"), lax.axis_index("gy")
    core = gx % 2
    z = (gx // 2) % 8
    base = gx - 2 * z
    core_peer = (base + 2 * z + 1 - 2 * core, gy)
    y_peer = ((gx + 16) % 32, gy)
    z_index = [(z + d) % 8 for d in range(1, 8)]
    z_peer = [(base + 2 * i, gy) for i in z_index]
    has_next, has_prev = gy < 7, gy > 0
    mode = core * 8 + z

    barrier = pltpu.get_barrier_semaphore()
    for peer in [core_peer, y_peer] + z_peer:
        pl.semaphore_signal(barrier, inc=1, device_id=peer, device_id_type=MESH)

    @pl.when(has_next)
    def _():
        pl.semaphore_signal(barrier, inc=1, device_id=(gx, gy + 1), device_id_type=MESH)

    @pl.when(has_prev)
    def _():
        pl.semaphore_signal(barrier, inc=1, device_id=(gx, gy - 1), device_id_type=MESH)

    loads = [pltpu.make_async_copy(f_hbm.at[:, y], fv.at[y + 1], fsem.at[y]) for y in range(YL)]
    for load in loads:
        load.start()
    others = [
        pltpu.make_async_copy(sw_hbm.at[mode], wmix, wsem.at[0]),
        pltpu.make_async_copy(w1_hbm, w1, wsem.at[1]),
        pltpu.make_async_copy(w2_hbm, w2, wsem.at[2]),
        pltpu.make_async_copy(b1_hbm, b1, wsem.at[3]),
        pltpu.make_async_copy(b2_hbm, b2, wsem.at[4]),
        pltpu.make_async_copy(taps_hbm, taps, wsem.at[5]),
    ]
    for load in others:
        load.start()

    tab[...] = table((2 * MODES, XL * Z), False)
    lane = lax.broadcasted_iota(jnp.int32, (8, XL * Z), 1) % 8
    own = (lane == lax.broadcasted_iota(jnp.int32, (8, XL * Z), 0)).astype(F32)
    for i in range(MODES):
        pair = [own * tab[2 * i + p : 2 * i + p + 1, :] for p in range(2)]
        fwd[16 * i : 16 * i + 16, :] = jnp.concatenate(pair, 0).astype(BF)

    for y in range(YL):
        loads[y].wait()
        s = jnp.dot(fwd[...], fv[y + 1].reshape(XL * Z, C), preferred_element_type=F32)
        s32[:, y] = s.reshape(MODES, 16, C)
    for k in range(8):
        csend[k] = s32[(1 - core) * 8 + k].astype(BF)

    pl.semaphore_wait(barrier, 9 + has_next.astype(jnp.int32) + has_prev.astype(jnp.int32))

    def to_next(c):
        rows = pl.ds(c * CROWS, CROWS)
        return pltpu.make_async_remote_copy(
            f_hbm.at[rows, YL - 1], fv.at[0, rows], hs.at[0, c], hr.at[0, c],
            device_id=(gx, gy + 1), device_id_type=MESH,
        )

    def to_prev(c):
        rows = pl.ds(c * CROWS, CROWS)
        return pltpu.make_async_remote_copy(
            f_hbm.at[rows, 0], fv.at[YL + 1, rows], hs.at[1, c], hr.at[1, c],
            device_id=(gx, gy - 1), device_id_type=MESH,
        )

    def send_halo(first, last):
        @pl.loop(first, last)
        def _(c):
            @pl.when(has_next)
            def _():
                to_next(c).start()

            @pl.when(has_prev)
            def _():
                to_prev(c).start()

    to_core = pltpu.make_async_remote_copy(csend, crecv, cs, cr, device_id=core_peer, device_id_type=MESH)
    to_core.start()
    send_halo(0, EARLY)
    to_core.wait()

    to_z = []
    for d in range(7):
        zo = z_index[d]
        zsend[d] = (s32[core * 8 + zo] + crecv[zo].astype(F32)).astype(BF)
        copy = pltpu.make_async_remote_copy(
            zsend.at[d], zrecv.at[d], zs.at[d], zr.at[d], device_id=z_peer[d], device_id_type=MESH
        )
        copy.start()
        to_z.append(copy)
    total = s32[mode] + crecv[z].astype(F32)

    tabt[...] = table((XL, C), True)
    lane = lax.broadcasted_iota(jnp.int32, (8, C), 1) % 8
    own = (lane == lax.broadcasted_iota(jnp.int32, (8, C), 0)).astype(F32)

    @pl.loop(0, XL // 8)
    def _(i):
        rows = tabt[pl.ds(pl.multiple_of(i * 8, 8), 8), :]
        spread = [own * rows[r : r + 1, :] for r in range(8)]
        inv[pl.ds(pl.multiple_of(i * 64, 64), 64), :] = jnp.concatenate(spread, 0).astype(BF)

    @pl.when(jnp.logical_not(has_prev))
    def _():
        fv[0] = jnp.zeros((XL, Z, C), BF)

    @pl.when(jnp.logical_not(has_next))
    def _():
        fv[YL + 1] = jnp.zeros((XL, Z, C), BF)

    for load in others:
        load.wait()
    for copy in to_z:
        copy.wait()
    for d in range(7):
        total = total + zrecv[d].astype(F32)

    ysend[...] = total.astype(BF)
    to_y = pltpu.make_async_remote_copy(ysend, yrecv, ys, yr, device_id=y_peer, device_id_type=MESH)
    to_y.start()
    send_halo(EARLY, NCH)
    to_y.wait()
    total = ysend[...].astype(F32) + yrecv[...].astype(F32)

    real = total[:, 0:8].reshape(YL * Z, C)
    imag = total[:, 8:16].reshape(YL * Z, C)
    both = jnp.concatenate([real, imag], 0).astype(BF)
    by_real = jnp.dot(both, wmix[0], preferred_element_type=F32)
    by_imag = jnp.dot(both, wmix[1], preferred_element_type=F32)
    n = YL * Z
    mixed_real = (by_real[:n] - by_imag[n:]).reshape(YL, 8, C)
    mixed_imag = (by_imag[:n] + by_real[n:]).reshape(YL, 8, C)
    result = jnp.concatenate([mixed_real, mixed_imag], 1).astype(BF)
    mixed[...] = result
    mg[:, mode] = result

    def to_all(d):
        return pltpu.make_async_remote_copy(
            mixed, mg.at[:, mode], gs.at[d], gr.at[d], device_id=z_peer[d], device_id_type=MESH
        )

    def from_z(d):
        zo = (z + 7 - d) % 8
        return pltpu.make_async_remote_copy(
            mixed, mg.at[:, core * 8 + zo], gs.at[d], gr.at[d], device_id=z_peer[d], device_id_type=MESH
        )

    def forward(src, slot, i):
        return pltpu.make_async_remote_copy(
            src, mg.at[:, slot], ks.at[i], kr.at[i], device_id=core_peer, device_id_type=MESH
        )

    order = [3, 2, 4, 1, 5, 0, 6]
    arrive = [0, 6, 1, 5, 2, 4, 3]
    for d in order:
        to_all(d).start()
    first = forward(mixed, mode, 7)
    first.start()
    relays = [first]
    for d in arrive:
        from_z(d).wait_recv()
        slot = core * 8 + (z + 7 - d) % 8
        relay = forward(mg.at[:, slot], slot, d)
        relay.start()
        relays.append(relay)
    for d in order:
        to_all(d).wait_send()
    for relay in relays:
        relay.wait()

    def mlp(joined, center):
        acc = center + b2[...]
        for h in range(0, HID, HC):
            hidden = jnp.dot(joined, w1[:, h : h + HC], preferred_element_type=F32) + b1[:, h : h + HC]
            hidden = gelu_doubled(hidden).astype(BF)
            acc = acc + 0.5 * jnp.dot(hidden, w2[h : h + HC, :], preferred_element_type=F32)
        return acc

    def joined_of(y, x0, cells):
        n = cells * Z
        rows = pl.ds(pl.multiple_of(x0 * Z, n), n)
        at = pl.ds(x0, cells)
        value = jnp.dot(inv[rows, :], mg[y].reshape(C, C), preferred_element_type=F32)
        near = [fv[y + i, at].reshape(n, C).astype(F32) for i in range(3)]
        conv = taps[0:1] * near[0] + taps[1:2] * near[1] + taps[2:3] * near[2]
        return (value + conv).astype(BF), near[1]

    per_row = XL // XB

    @pl.loop(0, 2 * per_row)
    def _(i):
        y = 1 + i // per_row
        x0 = pl.multiple_of((i % per_row) * XB, XB)
        joined, center = joined_of(y, x0, XB)
        out[pl.ds(x0, XB), y] = mlp(joined, center).astype(BF).reshape(XB, Z, C)

    per_block = HB // CROWS

    @pl.loop(0, XL // HB)
    def _(i):
        x0 = pl.multiple_of(i * HB, HB)

        @pl.loop(i * per_block, (i + 1) * per_block)
        def _(c):
            @pl.when(has_next)
            def _():
                to_next(c).wait_send()
                to_prev(c).wait_recv()

            @pl.when(has_prev)
            def _():
                to_prev(c).wait_send()
                to_next(c).wait_recv()

        low, low_center = joined_of(0, x0, HB)
        high, high_center = joined_of(YL - 1, x0, HB)
        value = mlp(jnp.concatenate([low, high], 0), jnp.concatenate([low_center, high_center], 0))
        value = value.astype(BF)
        out[pl.ds(x0, HB), 0] = value[: HB * Z].reshape(HB, Z, C)
        out[pl.ds(x0, HB), YL - 1] = value[HB * Z :].reshape(HB, Z, C)


def local(features, spectral_weight, conv_taps, w_in, bias_in, w_out, bias_out):
    dma = pltpu.SemaphoreType.DMA
    vm = pltpu.VMEM
    return pl.pallas_call(
        kernel,
        out_shape=jax.ShapeDtypeStruct((XL, YL, Z, C), BF),
        in_specs=[pl.BlockSpec(memory_space=pl.ANY)] * 7,
        out_specs=pl.BlockSpec(memory_space=pltpu.VMEM),
        scratch_shapes=[
            vm((YL + 2, XL, Z, C), BF),
            vm((2 * MODES * 8, XL * Z), BF),
            vm((XL * Z, C), BF),
            vm((2 * MODES, XL * Z), F32),
            vm((XL, C), F32),
            vm((MODES, YL, 16, C), F32),
            vm((8, YL, 16, C), BF),
            vm((8, YL, 16, C), BF),
            vm((7, YL, 16, C), BF),
            vm((7, YL, 16, C), BF),
            vm((YL, 16, C), BF),
            vm((YL, 16, C), BF),
            vm((2, C, C), BF),
            vm((YL, 16, C), BF),
            vm((YL, MODES, 16, C), BF),
            vm((3, C), F32),
            vm((C, HID), BF),
            vm((1, HID), F32),
            vm((HID, C), BF),
            vm((1, C), F32),
            dma((YL,)),
            dma((6,)),
            dma((2, NCH)),
            dma((2, NCH)),
            dma,
            dma,
            dma((7,)),
            dma((7,)),
            dma,
            dma,
            dma((7,)),
            dma((7,)),
            dma((8,)),
            dma((8,)),
        ],
        compiler_params=pltpu.CompilerParams(
            collective_id=0, has_side_effects=True, vmem_limit_bytes=56 << 20
        ),
        name="layer",
    )(
        features,
        spectral_weight,
        conv_taps,
        w_in,
        bias_in.reshape(1, HID),
        w_out,
        bias_out.reshape(1, C),
    )


def solution(mesh):
    return jax.shard_map(
        local,
        mesh=mesh,
        in_specs=(P("gx", "gy", None, None), P(), P(), P(), P(), P(), P()),
        out_specs=P("gx", "gy", None, None),
        check_vma=False,
    )
```

time: 121 us -> 74.4 us (0.61)
  the two profiles are of different devices: /device:TPU:6 before, /device:TPU:1 now
where the time goes in v1:
time: 74.4 us; the launch traced here: 74.3 us
  Pallas kernels  69.6 us (94%)
  local copies, waits for them, and re-layouts  4.64 us (6%)
    pallas_call x1, Pallas kernels, local(): pl.pallas_call(kernel, out_shape=jax.ShapeDtypeStruct((XL, YL, Z, C), BF)...  69.6 us
    unnamed x1, local copies, waits for them, and re-layouts  4.64 us

profile of v1, /device:TPU:1, one launch (start us, length us, event | category | flops | bytes accessed | tf_op | source)
XLA Modules:
  0.0 74.3 jit_solution(4375463110040804642)
XLA Ops:
  0.0 69.6 %layer.1 = bf16[256,4,8,256]{3,2,1,0:T(8,128)(2,1)} custom-call(bf16[256,4,8,256]{3,2,1,0:T(8,128)(2,1)} %f_hbm.1, bf16[16,2,256,256]{3,2,1,0:T(8,128)(2,1)} %sw_hbm.1, f32[3,256]{1,0:T(4,128)} %taps_hbm.1, bf16[256,1024]{1,0:T(8,128)(2,1)} %w1_hbm.1, f32[1,1024]{1,0:T(1,128)} %bitcast.2, bf16[1024,256]{1,0:T(8,128)(2,1)} %w2_hbm.1, f32[1,256]{1,0:T(1,128)} %bitcast.3), custom_call_target="tpu_custom_call" | custom-call | tf_op jit(solution)/shard_map/layer/pallas_call | solution.py:283
  69.6 4.6 %copy.9 = bf16[256,4,8,256]{3,2,1,0:T(8,128)(2,1)} copy(bf16[256,4,8,256]{3,2,1,0:T(8,128)(2,1)} %layer.1) | data formatting | bytes 8388608

commit v2 on v1

--- a/solution.py
+++ b/solution.py
@@ -19,10 +19,12 @@
 C = 256
 HID = 1024
 NCH = 16
-EARLY = 4
+EARLY = 5
 CROWS = XL // NCH
 XB = 128
 HB = 64
+RELAY = 12
+LAST = XL - HB
 HC = 256
 
 
@@ -47,11 +49,21 @@
     return x + x * t
 
 
+def mlp(joined, center, w1, b1, w2, b2):
+    acc = None
+    for h in range(0, HID, HC):
+        hidden = jnp.dot(joined, w1[:, h : h + HC], preferred_element_type=F32) + b1[:, h : h + HC]
+        hidden = gelu_doubled(hidden).astype(BF)
+        part = jnp.dot(hidden, w2[h : h + HC, :], preferred_element_type=F32)
+        acc = part if acc is None else acc + part
+    return center + b2[...] + 0.5 * acc
+
+
 def kernel(
     f_hbm, sw_hbm, taps_hbm, w1_hbm, b1_hbm, w2_hbm, b2_hbm,
-    out,
-    fv, fwd, inv, tab, tabt, s32, csend, crecv, zsend, zrecv, ysend, yrecv, wmix, mixed, mg, taps, w1, b1, w2, b2,
-    fsem, wsem, hs, hr, cs, cr, zs, zr, ys, yr, gs, gr, ks, kr,
+    out, last,
+    ov, jv, rl, fv, fwd, inv, tab, tabt, s32, csend, crecv, zsend, zrecv, ysend, yrecv, wmix, mixed, mg, taps, w1, b1, w2, b2,
+    fsem, wsem, hs, hr, cs, cr, zs, zr, ys, yr, gs, gr, ks, kr, rr, fs, osem,
 ):
     gx, gy = lax.axis_index("gx"), lax.axis_index("gy")
     core = gx % 2
@@ -61,20 +73,25 @@
     y_peer = ((gx + 16) % 32, gy)
     z_index = [(z + d) % 8 for d in range(1, 8)]
     z_peer = [(base + 2 * i, gy) for i in z_index]
+    mode = core * 8 + z
+    column, high = gy // 2, gy % 2
+    same = gy + 1 - 2 * high
+    diff = gy - 1 + 2 * high
     has_next, has_prev = gy < 7, gy > 0
-    mode = core * 8 + z
+    has_diff = (diff >= 0) & (diff <= 7)
+    from_low, from_high = gy > 1, gy < 6
+    relay_to = jnp.where(high == 0, gy + 2, gy - 2)
+    sent_by_relay = jnp.where(high == 1, 12 - 4 * column, 4 * column)
+    passed_on = jnp.where(high == 0, 12 - 4 * column, 4 * column)
 
     barrier = pltpu.get_barrier_semaphore()
-    for peer in [core_peer, y_peer] + z_peer:
+    for peer in [core_peer, y_peer, (gx, same)] + z_peer:
         pl.semaphore_signal(barrier, inc=1, device_id=peer, device_id_type=MESH)
-
-    @pl.when(has_next)
-    def _():
-        pl.semaphore_signal(barrier, inc=1, device_id=(gx, gy + 1), device_id_type=MESH)
-
-    @pl.when(has_prev)
-    def _():
-        pl.semaphore_signal(barrier, inc=1, device_id=(gx, gy - 1), device_id_type=MESH)
+    for there, peer in ((has_diff, diff), (from_low, gy - 2), (from_high, gy + 2)):
+
+        @pl.when(there)
+        def _():
+            pl.semaphore_signal(barrier, inc=1, device_id=(gx, peer), device_id_type=MESH)
 
     loads = [pltpu.make_async_copy(f_hbm.at[:, y], fv.at[y + 1], fsem.at[y]) for y in range(YL)]
     for load in loads:
@@ -104,32 +121,59 @@
     for k in range(8):
         csend[k] = s32[(1 - core) * 8 + k].astype(BF)
 
-    pl.semaphore_wait(barrier, 9 + has_next.astype(jnp.int32) + has_prev.astype(jnp.int32))
-
-    def to_next(c):
+    pl.semaphore_wait(barrier, 10 + sum(there.astype(jnp.int32) for there in (has_diff, from_low, from_high)))
+
+    row_same, slot_same = jnp.where(high == 0, YL - 1, 0), jnp.where(high == 0, 0, YL + 1)
+    row_diff, slot_diff = jnp.where(high == 1, YL - 1, 0), jnp.where(high == 1, 0, YL + 1)
+
+    def send_same(c):
         rows = pl.ds(c * CROWS, CROWS)
         return pltpu.make_async_remote_copy(
-            f_hbm.at[rows, YL - 1], fv.at[0, rows], hs.at[0, c], hr.at[0, c],
-            device_id=(gx, gy + 1), device_id_type=MESH,
-        )
-
-    def to_prev(c):
+            f_hbm.at[rows, row_same], fv.at[slot_same, rows], hs.at[0, c], hr.at[0, c],
+            device_id=(gx, same), device_id_type=MESH,
+        )
+
+    def send_diff(c):
         rows = pl.ds(c * CROWS, CROWS)
         return pltpu.make_async_remote_copy(
-            f_hbm.at[rows, 0], fv.at[YL + 1, rows], hs.at[1, c], hr.at[1, c],
-            device_id=(gx, gy - 1), device_id_type=MESH,
+            f_hbm.at[rows, row_diff], fv.at[slot_diff, rows], hs.at[1, c], hr.at[1, c],
+            device_id=(gx, diff), device_id_type=MESH,
+        )
+
+    def send_relay(c):
+        rows = pl.ds(c * CROWS, CROWS)
+        return pltpu.make_async_remote_copy(
+            f_hbm.at[rows, row_diff], rl.at[c], hs.at[1, c], rr.at[c],
+            device_id=(gx, same), device_id_type=MESH,
+        )
+
+    def pass_on(c):
+        rows = pl.ds(c * CROWS, CROWS)
+        return pltpu.make_async_remote_copy(
+            rl.at[c], fv.at[slot_same, rows], fs.at[c], hr.at[1, c],
+            device_id=(gx, relay_to), device_id_type=MESH,
         )
 
     def send_halo(first, last):
         @pl.loop(first, last)
         def _(c):
-            @pl.when(has_next)
+            send_same(c).start()
+
+            @pl.when(has_diff & (c < sent_by_relay))
             def _():
-                to_next(c).start()
-
-            @pl.when(has_prev)
+                send_relay(c).start()
+
+            @pl.when(has_diff & (c >= sent_by_relay))
             def _():
-                to_prev(c).start()
+                send_diff(c).start()
+
+    def relay_halo(first, last):
+        @pl.loop(first, last)
+        def _(c):
+            @pl.when(c < passed_on)
+            def _():
+                send_relay(c).wait_recv()
+                pass_on(c).start()
 
     to_core = pltpu.make_async_remote_copy(csend, crecv, cs, cr, device_id=core_peer, device_id_type=MESH)
     to_core.start()
@@ -137,7 +181,8 @@
     to_core.wait()
 
     to_z = []
-    for d in range(7):
+    order = [3, 2, 4, 1, 5, 0, 6]
+    for d in order:
         zo = z_index[d]
         zsend[d] = (s32[core * 8 + zo] + crecv[zo].astype(F32)).astype(BF)
         copy = pltpu.make_async_remote_copy(
@@ -207,10 +252,10 @@
             src, mg.at[:, slot], ks.at[i], kr.at[i], device_id=core_peer, device_id_type=MESH
         )
 
-    order = [3, 2, 4, 1, 5, 0, 6]
     arrive = [0, 6, 1, 5, 2, 4, 3]
     for d in order:
         to_all(d).start()
+    relay_halo(0, 4)
     first = forward(mixed, mode, 7)
     first.start()
     relays = [first]
@@ -225,13 +270,7 @@
     for relay in relays:
         relay.wait()
 
-    def mlp(joined, center):
-        acc = center + b2[...]
-        for h in range(0, HID, HC):
-            hidden = jnp.dot(joined, w1[:, h : h + HC], preferred_element_type=F32) + b1[:, h : h + HC]
-            hidden = gelu_doubled(hidden).astype(BF)
-            acc = acc + 0.5 * jnp.dot(hidden, w2[h : h + HC, :], preferred_element_type=F32)
-        return acc
+    relay_halo(4, 8)
 
     def joined_of(y, x0, cells):
         n = cells * Z
@@ -249,43 +288,101 @@
         y = 1 + i // per_row
         x0 = pl.multiple_of((i % per_row) * XB, XB)
         joined, center = joined_of(y, x0, XB)
-        out[pl.ds(x0, XB), y] = mlp(joined, center).astype(BF).reshape(XB, Z, C)
+        ov[pl.ds(x0, XB), y] = mlp(joined, center, w1, b1, w2, b2).astype(BF).reshape(XB, Z, C)
+
+    inner = pltpu.make_async_copy(ov.at[:, 1:3], out.at[:, 1:3], osem.at[0])
+    inner.start()
+    relay_halo(8, RELAY)
 
     per_block = HB // CROWS
 
-    @pl.loop(0, XL // HB)
-    def _(i):
+    def outer(i):
         x0 = pl.multiple_of(i * HB, HB)
 
         @pl.loop(i * per_block, (i + 1) * per_block)
         def _(c):
-            @pl.when(has_next)
+            send_same(c).wait()
+
+            @pl.when(has_diff)
             def _():
-                to_next(c).wait_send()
-                to_prev(c).wait_recv()
-
-            @pl.when(has_prev)
-            def _():
-                to_prev(c).wait_send()
-                to_next(c).wait_recv()
+                send_diff(c).wait()
 
         low, low_center = joined_of(0, x0, HB)
-        high, high_center = joined_of(YL - 1, x0, HB)
-        value = mlp(jnp.concatenate([low, high], 0), jnp.concatenate([low_center, high_center], 0))
-        value = value.astype(BF)
-        out[pl.ds(x0, HB), 0] = value[: HB * Z].reshape(HB, Z, C)
-        out[pl.ds(x0, HB), YL - 1] = value[HB * Z :].reshape(HB, Z, C)
+        high_, high_center = joined_of(YL - 1, x0, HB)
+        return jnp.concatenate([low, high_], 0), jnp.concatenate([low_center, high_center], 0)
+
+    def store(i, row, k):
+        rows = pl.ds(i * HB, HB)
+        return pltpu.make_async_copy(ov.at[rows, row], out.at[rows, row], osem.at[k])
+
+    @pl.loop(0, LAST // HB)
+    def _(i):
+        joined, center = outer(i)
+        value = mlp(joined, center, w1, b1, w2, b2).astype(BF)
+        rows = pl.ds(i * HB, HB)
+        ov[rows, 0] = value[: HB * Z].reshape(HB, Z, C)
+        ov[rows, YL - 1] = value[HB * Z :].reshape(HB, Z, C)
+        store(i, 0, 1 + 2 * i).start()
+        store(i, YL - 1, 2 + 2 * i).start()
+
+    jv[...] = outer(LAST // HB)[0]
+    final = pltpu.make_async_copy(jv, last, osem.at[7])
+    final.start()
+
+    @pl.loop(0, RELAY)
+    def _(c):
+        @pl.when(c < passed_on)
+        def _():
+            pass_on(c).wait_send()
+
+    inner.wait()
+    for i in range(LAST // HB):
+        store(i, 0, 1 + 2 * i).wait()
+        store(i, YL - 1, 2 + 2 * i).wait()
+    final.wait()
+
+
+def tail(part, f_hbm, joined_hbm, w1, b1, w2, b2, out, ov, fv, jv, isem, osem, jsem, fsem):
+    get_joined = pltpu.make_async_copy(joined_hbm, jv, jsem)
+    get_joined.start()
+    centers = [pltpu.make_async_copy(f_hbm.at[LAST:, (YL - 1) * i], fv.at[i], fsem.at[i]) for i in range(2)]
+    for copy in centers:
+        copy.start()
+    n = XL // HB
+    pieces = [slice(i * HB, (i + 1) * HB) for i in range(n)]
+    get = [pltpu.make_async_copy(part.at[p], ov.at[p], isem.at[i]) for i, p in enumerate(pieces[:-1])]
+    get.append(pltpu.make_async_copy(part.at[LAST:, 1:3], ov.at[LAST:, 1:3], isem.at[n - 1]))
+    put = [pltpu.make_async_copy(ov.at[p], out.at[p], osem.at[i]) for i, p in enumerate(pieces)]
+    for copy in get:
+        copy.start()
+    for i in range(n - 1):
+        get[i].wait()
+        put[i].start()
+    get_joined.wait()
+    for copy in centers:
+        copy.wait()
+    value = mlp(jv[...], fv[...].reshape(2 * HB * Z, C).astype(F32), w1, b1, w2, b2).astype(BF)
+    get[n - 1].wait()
+    ov[LAST:, 0] = value[: HB * Z].reshape(HB, Z, C)
+    ov[LAST:, YL - 1] = value[HB * Z :].reshape(HB, Z, C)
+    put[n - 1].start()
+    for copy in put:
+        copy.wait()
 
 
 def local(features, spectral_weight, conv_taps, w_in, bias_in, w_out, bias_out):
     dma = pltpu.SemaphoreType.DMA
     vm = pltpu.VMEM
-    return pl.pallas_call(
+    b1, b2 = bias_in.reshape(1, HID), bias_out.reshape(1, C)
+    part, last = pl.pallas_call(
         kernel,
-        out_shape=jax.ShapeDtypeStruct((XL, YL, Z, C), BF),
-        in_specs=[pl.BlockSpec(memory_space=pl.ANY)] * 7,
-        out_specs=pl.BlockSpec(memory_space=pltpu.VMEM),
+        out_shape=[jax.ShapeDtypeStruct((XL, YL, Z, C), BF), jax.ShapeDtypeStruct((2 * HB * Z, C), BF)],
+        in_specs=[pl.BlockSpec(memory_space=pltpu.HBM)] * 7,
+        out_specs=[pl.BlockSpec(memory_space=pl.ANY)] * 2,
         scratch_shapes=[
+            vm((XL, YL, Z, C), BF),
+            vm((2 * HB * Z, C), BF),
+            vm((RELAY, CROWS, Z, C), BF),
             vm((YL + 2, XL, Z, C), BF),
             vm((2 * MODES * 8, XL * Z), BF),
             vm((XL * Z, C), BF),
@@ -320,20 +417,34 @@
             dma((7,)),
             dma((8,)),
             dma((8,)),
+            dma((RELAY,)),
+            dma((RELAY,)),
+            dma((8,)),
         ],
         compiler_params=pltpu.CompilerParams(
-            collective_id=0, has_side_effects=True, vmem_limit_bytes=56 << 20
+            collective_id=0, has_side_effects=True, vmem_limit_bytes=36 << 20
         ),
         name="layer",
-    )(
-        features,
-        spectral_weight,
-        conv_taps,
-        w_in,
-        bias_in.reshape(1, HID),
-        w_out,
-        bias_out.reshape(1, C),
-    )
+    )(*[pltpu.with_memory_space_constraint(a, pltpu.HBM) for a in (features, spectral_weight, conv_taps, w_in, b1, w_out, b2)])
+    whole = pl.BlockSpec(memory_space=pltpu.VMEM)
+    hbm = pl.BlockSpec(memory_space=pl.ANY)
+    return pl.pallas_call(
+        tail,
+        out_shape=jax.ShapeDtypeStruct((XL, YL, Z, C), BF),
+        in_specs=[hbm, pl.BlockSpec(memory_space=pltpu.HBM), hbm] + [whole] * 4,
+        out_specs=hbm,
+        scratch_shapes=[
+            vm((XL, YL, Z, C), BF),
+            vm((2, HB, Z, C), BF),
+            vm((2 * HB * Z, C), BF),
+            dma((XL // HB,)),
+            dma((XL // HB,)),
+            dma,
+            dma((2,)),
+        ],
+        compiler_params=pltpu.CompilerParams(vmem_limit_bytes=24 << 20),
+        name="tail",
+    )(part, pltpu.with_memory_space_constraint(features, pltpu.HBM), last, w_in, b1, w_out, b2)
 
 
 def solution(mesh):

time: 74.4 us -> 68.5 us (0.921)
  the two profiles are of different devices: /device:TPU:1 before, /device:TPU:20 now
where the time goes in v2:
time: 68.5 us; the launch traced here: 68.4 us
  Pallas kernels  68.3 us (100%)
    pallas_call x1, Pallas kernels, local(): pl.pallas_call(kernel, out_shape=[jax.ShapeDtypeStruct((XL, YL, Z, C), BF...  64.4 us
    pallas_call x1, Pallas kernels, local(): pl.pallas_call(tail, out_shape=jax.ShapeDtypeStruct((XL, YL, Z, C), BF),...  3.94 us

profile of v2, /device:TPU:20, one launch (start us, length us, event | category | flops | bytes accessed | tf_op | source)
XLA Modules:
  0.0 68.4 jit_solution(9312696170420119807)
XLA Ops:
  0.0 0.0 copy-start
  0.0 0.0 copy-start.1
  0.0 0.0 copy-start.2
  0.0 0.0 copy-start.3
  0.0 64.4 %layer.1 = (bf16[256,4,8,256]{3,2,1,0:T(8,128)(2,1)S(1)}, bf16[1024,256]{1,0:T(8,128)(2,1)S(1)}) custom-call(bf16[256,4,8,256]{3,2,1,0:T(8,128)(2,1)} %f_hbm.3, bf16[16,2,256,256]{3,2,1,0:T(8,128)(2,1)} %sw_hbm.1, f32[3,256]{1,0:T(4,128)} %taps_hbm.1, bf16[256,1024]{1,0:T(8,128)(2,1)} %w1.1, f32[1,1024]{1,0:T(1,128)} %bitcast.2, bf16[1024,256]{1,0:T(8,128)(2,1)} %w2.1, ...), custom_call_target="tpu_custom_call" | custom-call | tf_op jit(solution)/shard_map/layer/pallas_call | solution.py:377
  64.4 0.0 copy-done
  64.4 0.0 copy-done.1
  64.5 0.0 copy-done.2
  64.5 0.0 copy-done.3
  64.5 3.9 %tail.1 = bf16[256,4,8,256]{3,2,1,0:T(8,128)(2,1)} custom-call(bf16[256,4,8,256]{3,2,1,0:T(8,128)(2,1)S(1)} %get-tuple-element.7.part, bf16[256,4,8,256]{3,2,1,0:T(8,128)(2,1)} %f_hbm.3, bf16[1024,256]{1,0:T(8,128)(2,1)S(1)} %get-tuple-element.8.joined_hbm, bf16[256,1024]{1,0:T(8,128)(2,1)S(1)} %copy-done, f32[1,1024]{1,0:T(1,128)S(1)} %bitcast.3, ...), custom_call_target="tpu_custom_call" | custom-call | tf_op jit(solution)/shard_map/tail/pallas_call | solution.py:431
Async XLA Ops:
  0.0 64.4 %copy-start = (bf16[256,1024]{1,0:T(8,128)(2,1)S(1)}, bf16[256,1024]{1,0:T(8,128)(2,1)}, u32[]{:S(2)}) copy-start(bf16[256,1024]{1,0:T(8,128)(2,1)} %w1.1) | copy-start | bytes 1572868
  0.0 64.4 %copy-start.1 = (bf16[1024,256]{1,0:T(8,128)(2,1)S(1)}, bf16[1024,256]{1,0:T(8,128)(2,1)}, u32[]{:S(2)}) copy-start(bf16[1024,256]{1,0:T(8,128)(2,1)} %w2.1) | copy-start | bytes 1572868
  0.0 64.5 %copy-start.2 = (f32[1024]{0:T(1024)S(1)}, f32[1024]{0:T(1024)}, u32[]{:S(2)}) copy-start(f32[1024]{0:T(1024)} %param.11) | copy-start | bytes 12292
  0.0 64.5 %copy-start.3 = (f32[256]{0:T(256)S(1)}, f32[256]{0:T(256)}, u32[]{:S(2)}) copy-start(f32[256]{0:T(256)} %param.13) | copy-start | bytes 3076

commit v3 on v2

--- a/solution.py
+++ b/solution.py
@@ -24,7 +24,8 @@
 XB = 128
 HB = 64
 RELAY = 12
-LAST = XL - HB
+TB = 32
+LAST = XL - TB
 HC = 256
 
 
@@ -154,18 +155,27 @@
             device_id=(gx, relay_to), device_id_type=MESH,
         )
 
+    def start_diff(c):
+        @pl.when(has_diff & (c < sent_by_relay))
+        def _():
+            send_relay(c).start()
+
+        @pl.when(has_diff & (c >= sent_by_relay))
+        def _():
+            send_diff(c).start()
+
     def send_halo(first, last):
         @pl.loop(first, last)
         def _(c):
             send_same(c).start()
 
-            @pl.when(has_diff & (c < sent_by_relay))
+            @pl.when(c < 12)
             def _():
-                send_relay(c).start()
-
-            @pl.when(has_diff & (c >= sent_by_relay))
+                start_diff(c + c // 3)
+
+            @pl.when((c < 12) & (c % 3 == 2))
             def _():
-                send_diff(c).start()
+                start_diff(c + c // 3 + 1)
 
     def relay_halo(first, last):
         @pl.loop(first, last)
@@ -220,8 +230,8 @@
     ysend[...] = total.astype(BF)
     to_y = pltpu.make_async_remote_copy(ysend, yrecv, ys, yr, device_id=y_peer, device_id_type=MESH)
     to_y.start()
+    to_y.wait()
     send_halo(EARLY, NCH)
-    to_y.wait()
     total = ysend[...].astype(F32) + yrecv[...].astype(F32)
 
     real = total[:, 0:8].reshape(YL * Z, C)
@@ -270,8 +280,6 @@
     for relay in relays:
         relay.wait()
 
-    relay_halo(4, 8)
-
     def joined_of(y, x0, cells):
         n = cells * Z
         rows = pl.ds(pl.multiple_of(x0 * Z, n), n)
@@ -281,25 +289,22 @@
         conv = taps[0:1] * near[0] + taps[1:2] * near[1] + taps[2:3] * near[2]
         return (value + conv).astype(BF), near[1]
 
-    per_row = XL // XB
-
-    @pl.loop(0, 2 * per_row)
-    def _(i):
-        y = 1 + i // per_row
-        x0 = pl.multiple_of((i % per_row) * XB, XB)
-        joined, center = joined_of(y, x0, XB)
-        ov[pl.ds(x0, XB), y] = mlp(joined, center, w1, b1, w2, b2).astype(BF).reshape(XB, Z, C)
-
+    def inner_row(y):
+        @pl.loop(0, XL // XB)
+        def _(i):
+            x0 = pl.multiple_of(i * XB, XB)
+            joined, center = joined_of(y, x0, XB)
+            ov[pl.ds(x0, XB), y] = mlp(joined, center, w1, b1, w2, b2).astype(BF).reshape(XB, Z, C)
+
+    inner_row(1)
+    relay_halo(4, 8)
+    inner_row(2)
     inner = pltpu.make_async_copy(ov.at[:, 1:3], out.at[:, 1:3], osem.at[0])
     inner.start()
     relay_halo(8, RELAY)
 
-    per_block = HB // CROWS
-
-    def outer(i):
-        x0 = pl.multiple_of(i * HB, HB)
-
-        @pl.loop(i * per_block, (i + 1) * per_block)
+    def outer(x0, cells):
+        @pl.loop(x0 // CROWS, (x0 + cells) // CROWS)
         def _(c):
             send_same(c).wait()
 
@@ -307,26 +312,34 @@
             def _():
                 send_diff(c).wait()
 
-        low, low_center = joined_of(0, x0, HB)
-        high_, high_center = joined_of(YL - 1, x0, HB)
+        low, low_center = joined_of(0, x0, cells)
+        high_, high_center = joined_of(YL - 1, x0, cells)
         return jnp.concatenate([low, high_], 0), jnp.concatenate([low_center, high_center], 0)
 
-    def store(i, row, k):
-        rows = pl.ds(i * HB, HB)
+    def store(x0, cells, row, k):
+        rows = pl.ds(x0, cells)
         return pltpu.make_async_copy(ov.at[rows, row], out.at[rows, row], osem.at[k])
 
-    @pl.loop(0, LAST // HB)
+    def outer_block(x0, cells, k):
+        joined, center = outer(x0, cells)
+        value = mlp(joined, center, w1, b1, w2, b2).astype(BF)
+        rows = pl.ds(x0, cells)
+        ov[rows, 0] = value[: cells * Z].reshape(cells, Z, C)
+        ov[rows, YL - 1] = value[cells * Z :].reshape(cells, Z, C)
+        store(x0, cells, 0, k).start()
+        store(x0, cells, YL - 1, k + 1).start()
+
+    wide = LAST // HB
+
+    @pl.loop(0, wide)
     def _(i):
-        joined, center = outer(i)
-        value = mlp(joined, center, w1, b1, w2, b2).astype(BF)
-        rows = pl.ds(i * HB, HB)
-        ov[rows, 0] = value[: HB * Z].reshape(HB, Z, C)
-        ov[rows, YL - 1] = value[HB * Z :].reshape(HB, Z, C)
-        store(i, 0, 1 + 2 * i).start()
-        store(i, YL - 1, 2 + 2 * i).start()
-
-    jv[...] = outer(LAST // HB)[0]
-    final = pltpu.make_async_copy(jv, last, osem.at[7])
+        outer_block(pl.multiple_of(i * HB, HB), HB, 1 + 2 * i)
+
+    outer_block(wide * HB, LAST - wide * HB, 1 + 2 * wide)
+
+    jv[...] = outer(LAST, TB)[0]
+    final = pltpu.make_async_copy(jv, last, osem.at[0])
+    inner.wait()
     final.start()
 
     @pl.loop(0, RELAY)
@@ -335,10 +348,11 @@
         def _():
             pass_on(c).wait_send()
 
-    inner.wait()
-    for i in range(LAST // HB):
-        store(i, 0, 1 + 2 * i).wait()
-        store(i, YL - 1, 2 + 2 * i).wait()
+    for i in range(wide):
+        store(i * HB, HB, 0, 1 + 2 * i).wait()
+        store(i * HB, HB, YL - 1, 2 + 2 * i).wait()
+    store(wide * HB, LAST - wide * HB, 0, 1 + 2 * wide).wait()
+    store(wide * HB, LAST - wide * HB, YL - 1, 2 + 2 * wide).wait()
     final.wait()
 
 
@@ -348,8 +362,9 @@
     centers = [pltpu.make_async_copy(f_hbm.at[LAST:, (YL - 1) * i], fv.at[i], fsem.at[i]) for i in range(2)]
     for copy in centers:
         copy.start()
-    n = XL // HB
-    pieces = [slice(i * HB, (i + 1) * HB) for i in range(n)]
+    cuts = [*range(0, LAST, HB), LAST, XL]
+    pieces = [slice(low, high) for low, high in zip(cuts, cuts[1:])]
+    n = len(pieces)
     get = [pltpu.make_async_copy(part.at[p], ov.at[p], isem.at[i]) for i, p in enumerate(pieces[:-1])]
     get.append(pltpu.make_async_copy(part.at[LAST:, 1:3], ov.at[LAST:, 1:3], isem.at[n - 1]))
     put = [pltpu.make_async_copy(ov.at[p], out.at[p], osem.at[i]) for i, p in enumerate(pieces)]
@@ -361,10 +376,10 @@
     get_joined.wait()
     for copy in centers:
         copy.wait()
-    value = mlp(jv[...], fv[...].reshape(2 * HB * Z, C).astype(F32), w1, b1, w2, b2).astype(BF)
+    value = mlp(jv[...], fv[...].reshape(2 * TB * Z, C).astype(F32), w1, b1, w2, b2).astype(BF)
     get[n - 1].wait()
-    ov[LAST:, 0] = value[: HB * Z].reshape(HB, Z, C)
-    ov[LAST:, YL - 1] = value[HB * Z :].reshape(HB, Z, C)
+    ov[LAST:, 0] = value[: TB * Z].reshape(TB, Z, C)
+    ov[LAST:, YL - 1] = value[TB * Z :].reshape(TB, Z, C)
     put[n - 1].start()
     for copy in put:
         copy.wait()
@@ -376,12 +391,12 @@
     b1, b2 = bias_in.reshape(1, HID), bias_out.reshape(1, C)
     part, last = pl.pallas_call(
         kernel,
-        out_shape=[jax.ShapeDtypeStruct((XL, YL, Z, C), BF), jax.ShapeDtypeStruct((2 * HB * Z, C), BF)],
+        out_shape=[jax.ShapeDtypeStruct((XL, YL, Z, C), BF), jax.ShapeDtypeStruct((2 * TB * Z, C), BF)],
         in_specs=[pl.BlockSpec(memory_space=pltpu.HBM)] * 7,
         out_specs=[pl.BlockSpec(memory_space=pl.ANY)] * 2,
         scratch_shapes=[
             vm((XL, YL, Z, C), BF),
-            vm((2 * HB * Z, C), BF),
+            vm((2 * TB * Z, C), BF),
             vm((RELAY, CROWS, Z, C), BF),
             vm((YL + 2, XL, Z, C), BF),
             vm((2 * MODES * 8, XL * Z), BF),
@@ -419,7 +434,7 @@
             dma((8,)),
             dma((RELAY,)),
             dma((RELAY,)),
-            dma((8,)),
+            dma((9,)),
         ],
         compiler_params=pltpu.CompilerParams(
             collective_id=0, has_side_effects=True, vmem_limit_bytes=36 << 20
@@ -435,10 +450,10 @@
         out_specs=hbm,
         scratch_shapes=[
             vm((XL, YL, Z, C), BF),
-            vm((2, HB, Z, C), BF),
-            vm((2 * HB * Z, C), BF),
-            dma((XL // HB,)),
-            dma((XL // HB,)),
+            vm((2, TB, Z, C), BF),
+            vm((2 * TB * Z, C), BF),
+            dma((XL // HB + 1,)),
+            dma((XL // HB + 1,)),
             dma,
             dma((2,)),
         ],

time: 68.5 us -> 59.5 us (0.87)
  the two profiles are of different devices: /device:TPU:20 before, /device:TPU:6 now
where the time goes in v3:
time: 59.5 us; the launch traced here: 59.4 us
  Pallas kernels  59.2 us (99%)
    pallas_call x1, Pallas kernels, local(): pl.pallas_call(kernel, out_shape=[jax.ShapeDtypeStruct((XL, YL, Z, C), BF...  56.3 us
    pallas_call x1, Pallas kernels, local(): pl.pallas_call(tail, out_shape=jax.ShapeDtypeStruct((XL, YL, Z, C), BF),...  2.92 us

profile of v3, /device:TPU:6, one launch (start us, length us, event | category | flops | bytes accessed | tf_op | source)
XLA Modules:
  0.0 59.4 jit_solution(4089953654771547051)
XLA Ops:
  0.0 0.0 copy-start
  0.0 0.0 copy-start.1
  0.0 0.0 copy-start.2
  0.0 0.0 copy-start.3
  0.0 56.3 %layer.1 = (bf16[256,4,8,256]{3,2,1,0:T(8,128)(2,1)S(1)}, bf16[512,256]{1,0:T(8,128)(2,1)S(1)}) custom-call(bf16[256,4,8,256]{3,2,1,0:T(8,128)(2,1)} %f_hbm.3, bf16[16,2,256,256]{3,2,1,0:T(8,128)(2,1)} %sw_hbm.1, f32[3,256]{1,0:T(4,128)} %taps_hbm.1, bf16[256,1024]{1,0:T(8,128)(2,1)} %w1.1, f32[1,1024]{1,0:T(1,128)} %bitcast.2, bf16[1024,256]{1,0:T(8,128)(2,1)} %w2.1, ...), custom_call_target="tpu_custom_call" | custom-call | tf_op jit(solution)/shard_map/layer/pallas_call | solution.py:392
  56.3 0.0 copy-done
  56.3 0.0 copy-done.1
  56.3 0.0 copy-done.2
  56.3 0.0 copy-done.3
  56.3 2.9 %tail.1 = bf16[256,4,8,256]{3,2,1,0:T(8,128)(2,1)} custom-call(bf16[256,4,8,256]{3,2,1,0:T(8,128)(2,1)S(1)} %get-tuple-element.7.part, bf16[256,4,8,256]{3,2,1,0:T(8,128)(2,1)} %f_hbm.3, bf16[512,256]{1,0:T(8,128)(2,1)S(1)} %get-tuple-element.8.joined_hbm, bf16[256,1024]{1,0:T(8,128)(2,1)S(1)} %copy-done, f32[1,1024]{1,0:T(1,128)S(1)} %bitcast.3, ...), custom_call_target="tpu_custom_call" | custom-call | tf_op jit(solution)/shard_map/tail/pallas_call | solution.py:446
Async XLA Ops:
  0.0 56.3 %copy-start = (bf16[256,1024]{1,0:T(8,128)(2,1)S(1)}, bf16[256,1024]{1,0:T(8,128)(2,1)}, u32[]{:S(2)}) copy-start(bf16[256,1024]{1,0:T(8,128)(2,1)} %w1.1) | copy-start | bytes 1572868
  0.0 56.3 %copy-start.1 = (bf16[1024,256]{1,0:T(8,128)(2,1)S(1)}, bf16[1024,256]{1,0:T(8,128)(2,1)}, u32[]{:S(2)}) copy-start(bf16[1024,256]{1,0:T(8,128)(2,1)} %w2.1) | copy-start | bytes 1572868
  0.0 56.3 %copy-start.2 = (f32[1024]{0:T(1024)S(1)}, f32[1024]{0:T(1024)}, u32[]{:S(2)}) copy-start(f32[1024]{0:T(1024)} %param.11) | copy-start | bytes 12292
  0.0 56.3 %copy-start.3 = (f32[256]{0:T(256)S(1)}, f32[256]{0:T(256)}, u32[]{:S(2)}) copy-start(f32[256]{0:T(256)} %param.13) | copy-start | bytes 3076

commit v4 on v3

v4 whole, which is shorter than its diff:
```python
import functools
import math

import jax
import jax.numpy as jnp
from jax import lax
from jax.experimental import pallas as pl
from jax.experimental.pallas import tpu as pltpu
from jax.sharding import PartitionSpec as P

MESH = pl.DeviceIdType.MESH
BF = jnp.bfloat16
F32 = jnp.float32
X = 8192
MODES = 16
XL = 256
YL = 4
Z = 8
C = 256
HID = 1024
NCH = 16
EARLY = 5
AHEAD = 2
CROWS = XL // NCH
XB = 128
HB = 64
RELAY = 12
TB = 16
LAST = XL - TB
HC = 256


def table(shape, lane_is_mode):
    rows = lax.broadcasted_iota(jnp.int32, shape, 0)
    cols = lax.broadcasted_iota(jnp.int32, shape, 1)
    first = lax.axis_index("gx") * XL
    if lane_is_mode:
        mode, part, x = cols // 16, (cols // 8) % 2, first + rows
    else:
        mode, part, x = rows // 2, rows % 2, first + cols // 8
    turn = (mode * x + part * (X // 4)) % X
    value = jnp.cos((2.0 * math.pi / X) * turn.astype(F32)) * (1.0 / math.sqrt(X))
    if lane_is_mode:
        value = value * jnp.where(mode == 0, 1.0, 2.0)
    return value


def gelu_doubled(x):
    c = math.sqrt(2.0 / math.pi)
    t = jnp.tanh(x * (c + (c * 0.044715) * (x * x)))
    return x + x * t


def mlp(joined, center, w1, b1, w2, b2):
    parts = []
    for h in range(0, HID, HC):
        hidden = jnp.dot(joined, w1[:, h : h + HC], preferred_element_type=F32) + b1[:, h : h + HC]
        parts.append(gelu_doubled(hidden).astype(BF))
    value = 0.5 * jnp.dot(jnp.concatenate(parts, 1), w2[...], preferred_element_type=F32) + b2[...]
    return value if center is None else value + center


def kernel(
    f_hbm, sw_hbm, taps_hbm, w1_hbm, b1_hbm, w2_hbm, b2_hbm,
    out, last,
    ov, jv, rl, fv, fwd, inv, tab, tabt, s32, csend, crecv, zsend, zrecv, ysend, yrecv, wmix, mixed, mg, taps, w1, b1, w2, b2,
    fsem, wsem, hs, hr, cs, cr, zs, zr, ys, yr, gs, gr, ks, kr, rr, fs, here, osem,
):
    gx, gy = lax.axis_index("gx"), lax.axis_index("gy")
    core = gx % 2
    z = (gx // 2) % 8
    base = gx - 2 * z
    core_peer = (base + 2 * z + 1 - 2 * core, gy)
    y_peer = ((gx + 16) % 32, gy)
    z_index = [(z + d) % 8 for d in range(1, 8)]
    z_peer = [(base + 2 * i, gy) for i in z_index]
    mode = core * 8 + z
    column, high = gy // 2, gy % 2
    same = gy + 1 - 2 * high
    diff = gy - 1 + 2 * high
    has_next, has_prev = gy < 7, gy > 0
    has_diff = (diff >= 0) & (diff <= 7)
    from_low, from_high = gy > 1, gy < 6
    relay_to = jnp.where(high == 0, gy + 2, gy - 2)
    sent_by_relay = jnp.where(high == 1, 12 - 4 * column, 4 * column)
    passed_on = jnp.where(high == 0, 12 - 4 * column, 4 * column)

    barrier = pltpu.get_barrier_semaphore()
    for peer in [core_peer, y_peer, (gx, same)]:
        pl.semaphore_signal(barrier, inc=1, device_id=peer, device_id_type=MESH)
    for there, peer in ((has_diff, diff), (from_low, gy - 2), (from_high, gy + 2)):

        @pl.when(there)
        def _():
            pl.semaphore_signal(barrier, inc=1, device_id=(gx, peer), device_id_type=MESH)

    for i, peer in zip(z_index, z_peer):

        @pl.when(i > z)
        def _():
            pl.semaphore_signal(barrier, inc=1, device_id=peer, device_id_type=MESH)

    loads = [pltpu.make_async_copy(f_hbm.at[:, y], fv.at[y + 1], fsem.at[y]) for y in range(YL)]
    for load in loads:
        load.start()
    others = [
        pltpu.make_async_copy(sw_hbm.at[mode], wmix, wsem.at[0]),
        pltpu.make_async_copy(w1_hbm, w1, wsem.at[1]),
        pltpu.make_async_copy(w2_hbm, w2, wsem.at[2]),
        pltpu.make_async_copy(b1_hbm, b1, wsem.at[3]),
        pltpu.make_async_copy(b2_hbm, b2, wsem.at[4]),
        pltpu.make_async_copy(taps_hbm, taps, wsem.at[5]),
    ]
    for load in others:
        load.start()

    tab[...] = table((2 * MODES, XL * Z), False)
    lane = lax.broadcasted_iota(jnp.int32, (8, XL * Z), 1) % 8
    own = (lane == lax.broadcasted_iota(jnp.int32, (8, XL * Z), 0)).astype(F32)
    for i in range(MODES):
        pair = [own * tab[2 * i + p : 2 * i + p + 1, :] for p in range(2)]
        fwd[16 * i : 16 * i + 16, :] = jnp.concatenate(pair, 0).astype(BF)

    row_same, slot_same = jnp.where(high == 0, YL - 1, 0), jnp.where(high == 0, 0, YL + 1)
    row_diff, slot_diff = jnp.where(high == 1, YL - 1, 0), jnp.where(high == 1, 0, YL + 1)

    def block_of(c):
        return c // 4 + c // (NCH - 1)

    def send_same(c):
        rows = pl.ds(c * CROWS, CROWS)
        return pltpu.make_async_remote_copy(
            f_hbm.at[rows, row_same], fv.at[slot_same, rows], hs.at[0], hr.at[0, block_of(c)],
            device_id=(gx, same), device_id_type=MESH,
        )

    def send_diff(c):
        rows = pl.ds(c * CROWS, CROWS)
        return pltpu.make_async_remote_copy(
            f_hbm.at[rows, row_diff], fv.at[slot_diff, rows], hs.at[1], hr.at[1, block_of(c)],
            device_id=(gx, diff), device_id_type=MESH,
        )

    def send_relay(c):
        rows = pl.ds(c * CROWS, CROWS)
        return pltpu.make_async_remote_copy(
            f_hbm.at[rows, row_diff], rl.at[c], hs.at[1], rr.at[c // 4],
            device_id=(gx, same), device_id_type=MESH,
        )

    def pass_on(c):
        rows = pl.ds(c * CROWS, CROWS)
        return pltpu.make_async_remote_copy(
            rl.at[c], fv.at[slot_same, rows], fs.at[c // 4], hr.at[1, block_of(c)],
            device_id=(gx, relay_to), device_id_type=MESH,
        )

    def start_diff(c):
        @pl.when(has_diff & (c < sent_by_relay))
        def _():
            send_relay(c).start()

        @pl.when(has_diff & (c >= sent_by_relay))
        def _():
            send_diff(c).start()

    def step_diff(c):
        @pl.when(c < 12)
        def _():
            start_diff(c + c // 3)

        @pl.when((c < 12) & (c % 3 == 2))
        def _():
            start_diff(c + c // 3 + 1)

    def send_halo(first, last):
        @pl.loop(first, last)
        def _(c):
            send_same(c).start()
            step_diff(c)

    def passed(g):
        rows = pl.ds(4 * g, 4)
        return pltpu.make_async_remote_copy(
            rl.at[rows], rl.at[rows], fs.at[g], rr.at[g], device_id=(gx, relay_to), device_id_type=MESH
        )

    def relay_halo(g):
        @pl.when(4 * g < passed_on)
        def _():
            passed(g).wait_recv()

            @pl.loop(4 * g, 4 * g + 4)
            def _(c):
                pass_on(c).start()

    def transform(y):
        loads[y].wait()
        s = jnp.dot(fwd[...], fv[y + 1].reshape(XL * Z, C), preferred_element_type=F32)
        s32[:, y] = s.reshape(MODES, 16, C)

    for y in range(AHEAD):
        transform(y)
    pl.semaphore_wait(barrier, 3 + z + sum(there.astype(jnp.int32) for there in (has_diff, from_low, from_high)))
    for i, peer in zip(z_index, z_peer):

        @pl.when(i < z)
        def _():
            pl.semaphore_signal(here, inc=1, device_id=peer, device_id_type=MESH)

    send_halo(0, EARLY)
    send_same(EARLY).start()
    for y in range(AHEAD, YL):
        transform(y)
    for k in range(8):
        csend[k] = s32[(1 - core) * 8 + k].astype(BF)

    to_core = pltpu.make_async_remote_copy(csend, crecv, cs, cr, device_id=core_peer, device_id_type=MESH)
    to_core.start()
    to_core.wait()


    @pl.when(z < 7)
    def _():
        pl.semaphore_wait(here, 7 - z)

    order = [3, 2, 4, 1, 5, 0, 6]
    for d in order:
        zo = z_index[d]
        zsend[d] = (s32[core * 8 + zo] + crecv[zo].astype(F32)).astype(BF)
        copy = pltpu.make_async_remote_copy(
            zsend.at[d], zrecv.at[d], zs, zr, device_id=z_peer[d], device_id_type=MESH
        )
        copy.start()
    total = s32[mode] + crecv[z].astype(F32)

    tabt[...] = table((XL, C), True)
    lane = lax.broadcasted_iota(jnp.int32, (8, C), 1) % 8
    own = (lane == lax.broadcasted_iota(jnp.int32, (8, C), 0)).astype(F32)

    @pl.loop(0, XL // 8)
    def _(i):
        rows = tabt[pl.ds(pl.multiple_of(i * 8, 8), 8), :]
        spread = [own * rows[r : r + 1, :] for r in range(8)]
        inv[pl.ds(pl.multiple_of(i * 64, 64), 64), :] = jnp.concatenate(spread, 0).astype(BF)

    @pl.when(jnp.logical_not(has_prev))
    def _():
        fv[0] = jnp.zeros((XL, Z, C), BF)

    @pl.when(jnp.logical_not(has_next))
    def _():
        fv[YL + 1] = jnp.zeros((XL, Z, C), BF)

    for load in others:
        load.wait()
    pltpu.make_async_remote_copy(zsend, zrecv, zs, zr, device_id=z_peer[0], device_id_type=MESH).wait()
    for d in range(7):
        total = total + zrecv[d].astype(F32)

    ysend[...] = total.astype(BF)
    to_y = pltpu.make_async_remote_copy(ysend, yrecv, ys, yr, device_id=y_peer, device_id_type=MESH)
    to_y.start()
    to_y.wait()
    step_diff(EARLY)
    send_halo(EARLY + 1, NCH)
    total = ysend[...].astype(F32) + yrecv[...].astype(F32)

    real = total[:, 0:8].reshape(YL * Z, C)
    imag = total[:, 8:16].reshape(YL * Z, C)
    both = jnp.concatenate([real, imag], 0).astype(BF)
    by_real = jnp.dot(both, wmix[0], preferred_element_type=F32)
    by_imag = jnp.dot(both, wmix[1], preferred_element_type=F32)
    n = YL * Z
    mixed_real = (by_real[:n] - by_imag[n:]).reshape(YL, 8, C)
    mixed_imag = (by_imag[:n] + by_real[n:]).reshape(YL, 8, C)
    result = jnp.concatenate([mixed_real, mixed_imag], 1).astype(BF)
    mixed[...] = result
    mg[:, mode] = result

    def to_all(d):
        return pltpu.make_async_remote_copy(
            mixed, mg.at[:, mode], gs, gr.at[d], device_id=z_peer[d], device_id_type=MESH
        )

    def from_z(d):
        zo = (z + 7 - d) % 8
        return pltpu.make_async_remote_copy(
            mixed, mg.at[:, core * 8 + zo], gs, gr.at[d], device_id=z_peer[d], device_id_type=MESH
        )

    def forward(src, slot):
        return pltpu.make_async_remote_copy(
            src, mg.at[:, slot], ks, kr, device_id=core_peer, device_id_type=MESH
        )

    arrive = [0, 6, 1, 5, 2, 4, 3]
    for d in order:
        to_all(d).start()
    relay_halo(0)
    first = forward(mixed, mode)
    first.start()
    for d in arrive:
        from_z(d).wait_recv()
        slot = core * 8 + (z + 7 - d) % 8
        relay = forward(mg.at[:, slot], slot)
        relay.start()
    relay_halo(1)
    pltpu.make_async_remote_copy(zsend, zrecv, gs, zr, device_id=z_peer[0], device_id_type=MESH).wait_send()
    half = mg.at[:, pl.ds(8 - core * 8, 8)]
    pltpu.make_async_remote_copy(half, half, ks, kr, device_id=core_peer, device_id_type=MESH).wait()

    def joined_of(y, x0, cells):
        n = cells * Z
        rows = pl.ds(pl.multiple_of(x0 * Z, n), n)
        at = pl.ds(x0, cells)
        value = jnp.dot(inv[rows, :], mg[y].reshape(C, C), preferred_element_type=F32)
        near = [fv[y + i, at].reshape(n, C).astype(F32) for i in range(3)]
        conv = taps[0:1] * near[0] + taps[1:2] * near[1] + taps[2:3] * near[2]
        return (value + conv).astype(BF), near[1]

    per_row = XL // XB

    @pl.loop(0, 2 * per_row)
    def _(i):
        y = 1 + i // per_row
        x0 = pl.multiple_of((i % per_row) * XB, XB)
        joined, center = joined_of(y, x0, XB)
        ov[pl.ds(x0, XB), y] = mlp(joined, center, w1, b1, w2, b2).astype(BF).reshape(XB, Z, C)

        @pl.when(i == 1)
        def _():
            relay_halo(2)

    inner = pltpu.make_async_copy(ov.at[:, 1:3], out.at[:, 1:3], osem.at[0])
    inner.start()

    def halo_bytes(stream, row, x0, cells, block):
        at = pl.ds(x0, cells)
        return pltpu.make_async_remote_copy(
            f_hbm.at[at, row], fv.at[0, at], hs.at[stream], hr.at[stream, block],
            device_id=(gx, same), device_id_type=MESH,
        )

    def arrived(x0, cells, block):
        halo_bytes(0, row_same, x0, cells, block).wait_recv()

        @pl.when(has_diff)
        def _():
            halo_bytes(1, row_diff, x0, cells, block).wait_recv()

    def outer(x0, cells, block):
        arrived(x0, cells, block)
        low, low_center = joined_of(0, x0, cells)
        high_, high_center = joined_of(YL - 1, x0, cells)
        return jnp.concatenate([low, high_], 0), jnp.concatenate([low_center, high_center], 0)

    def store(x0, cells, i):
        rows, row = pl.ds(x0, cells), (YL - 1) * i
        return pltpu.make_async_copy(ov.at[rows, row], out.at[rows, row], osem.at[1 + i])

    def outer_block(x0, cells, block):
        joined, center = outer(x0, cells, block)
        value = mlp(joined, center, w1, b1, w2, b2).astype(BF)
        rows = pl.ds(x0, cells)
        ov[rows, 0] = value[: cells * Z].reshape(cells, Z, C)
        ov[rows, YL - 1] = value[cells * Z :].reshape(cells, Z, C)
        for i in range(2):
            store(x0, cells, i).start()

    wide = LAST // HB

    @pl.loop(0, wide)
    def _(i):
        outer_block(pl.multiple_of(i * HB, HB), HB, i)

    outer_block(wide * HB, LAST - wide * HB, wide)

    at, n = slice(LAST, XL), TB * Z
    parts = []
    for y, other in ((0, 2), (YL - 1, YL - 1)):
        value = jnp.dot(inv[LAST * Z :, :], mg[y].reshape(C, C), preferred_element_type=F32)
        for slot in (y + 1, other):
            value = value + taps[slot - y : slot - y + 1] * fv[slot, at].reshape(n, C).astype(F32)
        parts.append(value)
    arrived(LAST, TB, wide + 1)
    low_halo = taps[0:1] * fv[0, at].reshape(n, C).astype(F32)
    high_halo = taps[2:3] * fv[YL + 1, at].reshape(n, C).astype(F32)
    jv[:n] = (parts[0] + low_halo).astype(BF)
    jv[n:] = (parts[1] + high_halo).astype(BF)
    final = pltpu.make_async_copy(jv, last, osem.at[3])
    final.start()

    for g in range(RELAY // 4):

        @pl.when(4 * g < passed_on)
        def _():
            passed(g).wait_send()

    halo_bytes(0, row_same, 0, XL, 0).wait_send()

    @pl.when(has_diff)
    def _():
        halo_bytes(1, row_diff, 0, XL, 0).wait_send()

    inner.wait()
    for i in range(2):
        store(0, LAST, i).wait()
    final.wait()


def tail(part, f_hbm, joined, w1, b1, w2, b2, out, fv, rv, osem, fsem):
    rows = (slice(0, LAST), slice(0, YL)), (slice(LAST, XL), slice(1, YL - 1))
    put = [pltpu.make_async_copy(part.at[at], out.at[at], osem.at[i]) for i, at in enumerate(rows)]
    centers = [pltpu.make_async_copy(f_hbm.at[LAST:, (YL - 1) * i], fv.at[i], fsem.at[i]) for i in range(2)]
    for copy in centers + put:
        copy.start()
    value = mlp(joined[...], None, w1, b1, w2, b2)
    for copy in centers:
        copy.wait()
    value = value + fv[...].reshape(2 * TB * Z, C).astype(F32)
    rv[...] = value.astype(BF).reshape(2, TB, Z, C)
    for i in range(2):
        copy = pltpu.make_async_copy(rv.at[i], out.at[LAST:, (YL - 1) * i], osem.at[2 + i])
        copy.start()
        put.append(copy)
    for copy in put:
        copy.wait()


def local(features, spectral_weight, conv_taps, w_in, bias_in, w_out, bias_out):
    dma = pltpu.SemaphoreType.DMA
    vm = pltpu.VMEM
    b1, b2 = bias_in.reshape(1, HID), bias_out.reshape(1, C)
    part, last = pl.pallas_call(
        kernel,
        out_shape=[jax.ShapeDtypeStruct((XL, YL, Z, C), BF), jax.ShapeDtypeStruct((2 * TB * Z, C), BF)],
        in_specs=[pl.BlockSpec(memory_space=pltpu.HBM)] * 7,
        out_specs=[pl.BlockSpec(memory_space=pl.ANY)] * 2,
        scratch_shapes=[
            vm((XL, YL, Z, C), BF),
            vm((2 * TB * Z, C), BF),
            vm((RELAY, CROWS, Z, C), BF),
            vm((YL + 2, XL, Z, C), BF),
            vm((2 * MODES * 8, XL * Z), BF),
            vm((XL * Z, C), BF),
            vm((2 * MODES, XL * Z), F32),
            vm((XL, C), F32),
            vm((MODES, YL, 16, C), F32),
            vm((8, YL, 16, C), BF),
            vm((8, YL, 16, C), BF),
            vm((7, YL, 16, C), BF),
            vm((7, YL, 16, C), BF),
            vm((YL, 16, C), BF),
            vm((YL, 16, C), BF),
            vm((2, C, C), BF),
            vm((YL, 16, C), BF),
            vm((YL, MODES, 16, C), BF),
            vm((3, C), F32),
            vm((C, HID), BF),
            vm((1, HID), F32),
            vm((HID, C), BF),
            vm((1, C), F32),
            dma((YL,)),
            dma((6,)),
            dma((2,)),
            dma((2, XL // HB + 1)),
            dma,
            dma,
            dma,
            dma,
            dma,
            dma,
            dma,
            dma((7,)),
            dma,
            dma,
            dma((RELAY // 4,)),
            dma((RELAY // 4,)),
            pltpu.SemaphoreType.REGULAR,
            dma((4,)),
        ],
        compiler_params=pltpu.CompilerParams(
            collective_id=0, has_side_effects=True, vmem_limit_bytes=36 << 20
        ),
        name="layer",
    )(*[pltpu.with_memory_space_constraint(a, pltpu.HBM) for a in (features, spectral_weight, conv_taps, w_in, b1, w_out, b2)])
    whole = pl.BlockSpec(memory_space=pltpu.VMEM)
    hbm = pl.BlockSpec(memory_space=pl.ANY)
    return pl.pallas_call(
        tail,
        out_shape=jax.ShapeDtypeStruct((XL, YL, Z, C), BF),
        in_specs=[hbm, hbm] + [whole] * 5,
        out_specs=hbm,
        scratch_shapes=[
            vm((2, TB, Z, C), BF),
            vm((2, TB, Z, C), BF),
            dma((4,)),
            dma((2,)),
        ],
        compiler_params=pltpu.CompilerParams(vmem_limit_bytes=24 << 20),
        name="tail",
    )(part, pltpu.with_memory_space_constraint(features, pltpu.HBM), last, w_in, b1, w_out, b2)


def solution(mesh):
    return jax.shard_map(
        local,
        mesh=mesh,
        in_specs=(P("gx", "gy", None, None), P(), P(), P(), P(), P(), P()),
        out_specs=P("gx", "gy", None, None),
        check_vma=False,
    )
```

time: 59.5 us -> 57.4 us (0.965)
  Pallas kernels: 59.2 us -> 57.2 us
    pallas_call x1, Pallas kernels: 56.3 us -> 55 us  [local(): pl.pallas_call(kernel, out_shape=[jax.ShapeDtypeStruct((XL, YL, Z, C), BF...]
    pallas_call x1, Pallas kernels: 2.92 us -> 2.2 us  [local(): pl.pallas_call(tail, out_shape=jax.ShapeDtypeStruct((XL, YL, Z, C), BF),...]
where the time goes in v4:
time: 57.4 us; the launch traced here: 57.2 us
  Pallas kernels  57.2 us (100%)
    pallas_call x1, Pallas kernels, local(): pl.pallas_call(kernel, out_shape=[jax.ShapeDtypeStruct((XL, YL, Z, C), BF...  55 us
    pallas_call x1, Pallas kernels, local(): pl.pallas_call(tail, out_shape=jax.ShapeDtypeStruct((XL, YL, Z, C), BF),...  2.2 us

profile of v4, /device:TPU:6, one launch (start us, length us, event | category | flops | bytes accessed | tf_op | source)
XLA Modules:
  0.0 57.2 jit_solution(2751394919844877215)
XLA Ops:
  0.0 0.0 copy-start
  0.0 0.0 copy-start.1
  0.0 0.0 copy-start.2
  0.0 0.0 copy-start.3
  0.0 55.0 %layer.1 = (bf16[256,4,8,256]{3,2,1,0:T(8,128)(2,1)S(1)}, bf16[256,256]{1,0:T(8,128)(2,1)S(1)}) custom-call(bf16[256,4,8,256]{3,2,1,0:T(8,128)(2,1)} %f_hbm.3, bf16[16,2,256,256]{3,2,1,0:T(8,128)(2,1)} %sw_hbm.1, f32[3,256]{1,0:T(4,128)} %taps_hbm.1, bf16[256,1024]{1,0:T(8,128)(2,1)} %w1.1, f32[1,1024]{1,0:T(1,128)} %bitcast.2, bf16[1024,256]{1,0:T(8,128)(2,1)} %w2.1, ...), custom_call_target="tpu_custom_call" | custom-call | tf_op jit(solution)/shard_map/layer/pallas_call | solution.py:435
  55.0 0.0 copy-done
  55.0 0.0 copy-done.1
  55.0 0.0 copy-done.2
  55.0 0.0 copy-done.3
  55.0 2.2 %tail.1 = bf16[256,4,8,256]{3,2,1,0:T(8,128)(2,1)} custom-call(bf16[256,4,8,256]{3,2,1,0:T(8,128)(2,1)S(1)} %get-tuple-element.7.part, bf16[256,4,8,256]{3,2,1,0:T(8,128)(2,1)} %f_hbm.3, bf16[256,256]{1,0:T(8,128)(2,1)S(1)} %get-tuple-element.8.joined, bf16[256,1024]{1,0:T(8,128)(2,1)S(1)} %copy-done, f32[1,1024]{1,0:T(1,128)S(1)} %bitcast.3, ...), custom_call_target="tpu_custom_call" | custom-call | tf_op jit(solution)/shard_map/tail/pallas_call | solution.py:490
Async XLA Ops:
  0.0 55.0 %copy-start = (bf16[256,1024]{1,0:T(8,128)(2,1)S(1)}, bf16[256,1024]{1,0:T(8,128)(2,1)}, u32[]{:S(2)}) copy-start(bf16[256,1024]{1,0:T(8,128)(2,1)} %w1.1) | copy-start | bytes 1572868
  0.0 55.0 %copy-start.1 = (bf16[1024,256]{1,0:T(8,128)(2,1)S(1)}, bf16[1024,256]{1,0:T(8,128)(2,1)}, u32[]{:S(2)}) copy-start(bf16[1024,256]{1,0:T(8,128)(2,1)} %w2.1) | copy-start | bytes 1572868
  0.0 55.0 %copy-start.2 = (f32[1024]{0:T(1024)S(1)}, f32[1024]{0:T(1024)}, u32[]{:S(2)}) copy-start(f32[1024]{0:T(1024)} %param.11) | copy-start | bytes 12292
  0.0 55.0 %copy-start.3 = (f32[256]{0:T(256)S(1)}, f32[256]{0:T(256)}, u32[]{:S(2)}) copy-start(f32[256]{0:T(256)} %param.13) | copy-start | bytes 3076

commit v5 on v4

--- a/solution.py
+++ b/solution.py
@@ -210,6 +210,7 @@
 
     send_halo(0, EARLY)
     send_same(EARLY).start()
+    start_diff(EARLY + EARLY // 3)
     for y in range(AHEAD, YL):
         transform(y)
     for k in range(8):
@@ -262,7 +263,7 @@
     to_y = pltpu.make_async_remote_copy(ysend, yrecv, ys, yr, device_id=y_peer, device_id_type=MESH)
     to_y.start()
     to_y.wait()
-    step_diff(EARLY)
+    start_diff(EARLY + EARLY // 3 + 1)
     send_halo(EARLY + 1, NCH)
     total = ysend[...].astype(F32) + yrecv[...].astype(F32)
 

time: 57.4 us -> 56.7 us (0.988)
  Pallas kernels: 57.2 us -> 56 us
    pallas_call x1, Pallas kernels: 55 us -> 53.8 us  [local(): pl.pallas_call(kernel, out_shape=[jax.ShapeDtypeStruct((XL, YL, Z, C), BF...]
where the time goes in v5:
time: 56.7 us; the launch traced here: 56 us
  Pallas kernels  56 us (99%)
    pallas_call x1, Pallas kernels, local(): pl.pallas_call(kernel, out_shape=[jax.ShapeDtypeStruct((XL, YL, Z, C), BF...  53.8 us
    pallas_call x1, Pallas kernels, local(): pl.pallas_call(tail, out_shape=jax.ShapeDtypeStruct((XL, YL, Z, C), BF),...  2.2 us

profile of v5, /device:TPU:6, one launch (start us, length us, event | category | flops | bytes accessed | tf_op | source)
XLA Modules:
  0.0 56.0 jit_solution(1214188813039959636)
XLA Ops:
  0.0 0.0 copy-start
  0.0 0.0 copy-start.1
  0.0 0.0 copy-start.2
  0.0 0.0 copy-start.3
  0.0 53.8 %layer.1 = (bf16[256,4,8,256]{3,2,1,0:T(8,128)(2,1)S(1)}, bf16[256,256]{1,0:T(8,128)(2,1)S(1)}) custom-call(bf16[256,4,8,256]{3,2,1,0:T(8,128)(2,1)} %f_hbm.3, bf16[16,2,256,256]{3,2,1,0:T(8,128)(2,1)} %sw_hbm.1, f32[3,256]{1,0:T(4,128)} %taps_hbm.1, bf16[256,1024]{1,0:T(8,128)(2,1)} %w1.1, f32[1,1024]{1,0:T(1,128)} %bitcast.2, bf16[1024,256]{1,0:T(8,128)(2,1)} %w2.1, ...), custom_call_target="tpu_custom_call" | custom-call | tf_op jit(solution)/shard_map/layer/pallas_call | solution.py:436
  53.8 0.0 copy-done
  53.8 0.0 copy-done.1
  53.8 0.0 copy-done.2
  53.8 0.0 copy-done.3
  53.8 2.2 %tail.1 = bf16[256,4,8,256]{3,2,1,0:T(8,128)(2,1)} custom-call(bf16[256,4,8,256]{3,2,1,0:T(8,128)(2,1)S(1)} %get-tuple-element.7.part, bf16[256,4,8,256]{3,2,1,0:T(8,128)(2,1)} %f_hbm.3, bf16[256,256]{1,0:T(8,128)(2,1)S(1)} %get-tuple-element.8.joined, bf16[256,1024]{1,0:T(8,128)(2,1)S(1)} %copy-done, f32[1,1024]{1,0:T(1,128)S(1)} %bitcast.3, ...), custom_call_target="tpu_custom_call" | custom-call | tf_op jit(solution)/shard_map/tail/pallas_call | solution.py:491
Async XLA Ops:
  0.0 53.8 %copy-start = (bf16[256,1024]{1,0:T(8,128)(2,1)S(1)}, bf16[256,1024]{1,0:T(8,128)(2,1)}, u32[]{:S(2)}) copy-start(bf16[256,1024]{1,0:T(8,128)(2,1)} %w1.1) | copy-start | bytes 1572868
  0.0 53.8 %copy-start.1 = (bf16[1024,256]{1,0:T(8,128)(2,1)S(1)}, bf16[1024,256]{1,0:T(8,128)(2,1)}, u32[]{:S(2)}) copy-start(bf16[1024,256]{1,0:T(8,128)(2,1)} %w2.1) | copy-start | bytes 1572868
  0.0 53.8 %copy-start.2 = (f32[1024]{0:T(1024)S(1)}, f32[1024]{0:T(1024)}, u32[]{:S(2)}) copy-start(f32[1024]{0:T(1024)} %param.11) | copy-start | bytes 12292
  0.0 53.8 %copy-start.3 = (f32[256]{0:T(256)S(1)}, f32[256]{0:T(256)}, u32[]{:S(2)}) copy-start(f32[256]{0:T(256)} %param.13) | copy-start | bytes 3076
